TPU v7x, 32 devices: a whole 2x2x4 slice. The times are simulated.
32 devices in a mesh: shard: 8 (over y, x, core), rep: 4 (over z).
Axes of the slice: x: 2, y: 2, z: 4, core: 2. Of those that a mesh axis runs over, the one named last changes fastest.
Arguments:
- grad_parts: bfloat16 [4, 512, 8192], P('rep', 'shard'), may hold values from -12 to 12
- owner_plan: int32 [4, 4], P('rep'), may hold values from 0 to 7, as said below
- refresh: int32 [4, 2], P('rep'), may hold values from 0 to 7, as said below
- roots: bfloat16 [4, 8, 2, 512, 512], P('rep', 'shard'), may hold values from -0.02 to 0.52
Outputs:
- update: bfloat16 [512, 8192], P('shard', 'rep')
Inputs may be any that keep to these rules, and one draw needn't show every extreme that they name: `owner_plan`: within each replica's row the 4 owners are distinct; otherwise the assignment is arbitrary. `refresh`: entry 2 b + s names side s (0 left, 1 right) of block b of the row's replica; no block appears twice in a row.
All inputs are finite; a program needn't handle non-finite values.
Results may differ from a plain program's by a relative error of at most 0.018.
Values may be sent and summed in bfloat16 or wider, within the bound.
A program may use at most 64 MiB of HBM per device.

v0:
```python
import jax
import jax.numpy as jnp
from jax import lax
from jax.sharding import PartitionSpec as P

NEWTON = 2


damping = 0.1


def product(first_mat, second_mat):
    return jnp.dot(
        first_mat, second_mat, precision=lax.Precision.HIGHEST, preferred_element_type=jnp.float32
    )


def inverse_root(statistic):
    matrix_size = statistic.shape[0]
    identity = jnp.eye(matrix_size, dtype=jnp.float32)
    damped = statistic + (damping * jnp.trace(statistic) / matrix_size + 1e-06) * identity
    norm_scale = 2.5 / jnp.sqrt(jnp.sum(damped * damped))
    current = identity * jnp.sqrt(jnp.sqrt(norm_scale))
    moment = damped * norm_scale
    for repeat in range(NEWTON):
        factor = (5.0 * identity - moment) * 0.25
        current = product(current, factor)
        square = product(factor, factor)
        moment = product(square, product(square, moment))
    return current.astype(jnp.bfloat16)


def local(grad_parts, owner_plan, refresh, roots):
    shards = lax.axis_size("shard")
    block_width = roots.shape[-1]
    partial_value = grad_parts[0].astype(jnp.float32)
    row_dev = partial_value.shape[0]
    my_columns = lax.psum_scatter(
        partial_value.astype(jnp.bfloat16), "rep", scatter_dimension=1, tiled=True
    )
    owner_row = owner_plan[0]
    block_count = owner_row.shape[0]
    pieces = my_columns.reshape(row_dev, block_count, block_width)
    targets = (owner_row[None, :] == jnp.arange(shards, dtype=jnp.int32)[:, None]).astype(
        jnp.bfloat16
    )
    outgoing = jnp.einsum(
        "ob,rbc->orc", targets, pieces, preferred_element_type=jnp.float32
    ).astype(jnp.bfloat16)
    incoming = lax.all_to_all(outgoing, "shard", split_axis=0, concat_axis=1, tiled=True)
    grad_block = incoming[0]
    my_index = lax.axis_index("shard")
    is_owner = owner_row == my_index
    has_block = jnp.any(is_owner)
    local_id = jnp.sum(jnp.where(is_owner, jnp.arange(block_count, dtype=jnp.int32), 0))
    refresh_row = refresh[0]
    stored = roots[0, 0]
    left_new = jnp.logical_and(has_block, jnp.any(refresh_row == 2 * local_id))
    right_new = jnp.logical_and(has_block, jnp.any(refresh_row == 2 * local_id + 1))

    def precondition():
        left_stat = lax.dot_general(
            grad_block, grad_block, (((1,), (1,)), ((), ())), preferred_element_type=jnp.float32
        )
        right_stat = lax.dot_general(
            grad_block, grad_block, (((0,), (0,)), ((), ())), preferred_element_type=jnp.float32
        )
        root_left = lax.cond(left_new, lambda: inverse_root(left_stat), lambda: stored[0])
        root_right = lax.cond(right_new, lambda: inverse_root(right_stat), lambda: stored[1])
        left_part = jnp.dot(root_left, grad_block, preferred_element_type=jnp.float32).astype(
            jnp.bfloat16
        )
        precon = jnp.dot(left_part, root_right, preferred_element_type=jnp.float32)
        values = grad_block.astype(jnp.float32)
        graft_scale = jnp.sqrt(
            (jnp.mean(values * values) + 1e-06) / (jnp.mean(precon * precon) + 1e-06)
        )
        return (precon * graft_scale).astype(jnp.bfloat16)

    def nothing():
        return jnp.zeros((block_width, block_width), jnp.bfloat16)

    update_block = lax.cond(has_block, precondition, nothing)
    returned = lax.all_to_all(
        update_block.reshape(shards, row_dev, block_width),
        "shard",
        split_axis=0,
        concat_axis=0,
        tiled=True,
    )
    placed = jnp.einsum(
        "ob,orc->rbc", targets, returned, preferred_element_type=jnp.float32
    ).astype(jnp.bfloat16)
    return placed.reshape(row_dev, block_count * block_width)


def solution(mesh):
    placed = (
        P("rep", "shard", None),
        P("rep", None),
        P("rep", None),
        P("rep", "shard", None, None, None),
    )
    return jax.shard_map(
        local, mesh=mesh, in_specs=placed, out_specs=P("shard", "rep"), check_vma=False
    )
```

profile of v0, /device:TPU:0, one launch (start us, length us, event | category | flops | bytes accessed | tf_op | source)
XLA Modules:
  0.0 101.4 jit_solution(11895012996952795628)
XLA Ops:
  6.5 0.0 reduce-scatter.2.cloned.1.call-start
  6.5 0.7 reduce-scatter.2.cloned.1.call-update
  7.3 32.4 %reduce-scatter.2.cloned.1.call-done = bf16[64,2048]{1,0:T(8,128)(2,1)} async-done(((bf16[64,8192]{1,0:T(8,128)(2,1)}), bf16[64,2048]{1,0:T(8,128)(2,1)}) %reduce-scatter.2.cloned.1.call-update) | async-done | bytes 262160 | tf_op jit(solution)/shard_map/reduce_scatter | solution.py:38
  39.7 1.1 %reshape.17 = bf16[64,4,512]{2,1,0:T(4,128)(2,1)S(1)} reshape(bf16[64,2048]{1,0:T(8,128)(2,1)} %reduce-scatter.2.cloned.1.call-done) | data formatting | bytes 524288 | tf_op jit(solution)/shard_map/reshape | solution.py:43
  40.8 0.0 copy-start.3
  40.8 0.6 copy-done.3
  41.5 0.4 convolution_convert_fusion.3
  41.9 0.0 copy-start
  41.9 0.9 copy.10
  42.8 3.7 %all-to-all-start = ((bf16[8,64,512]{2,1,0:T(8,128)(2,1)}), bf16[8,64,512]{2,1,0:T(8,128)(2,1)S(1)}, u32[]{:S(2)}, u32[]{:S(2)}) async-start(bf16[8,64,512]{2,1,0:T(8,128)(2,1)} %copy.10), calls=%async_computation.1 | async-start | bytes 1048576 | tf_op jit(solution)/shard_map/all_to_all | solution.py:50
  46.5 0.6 fusion.59
  47.8 8.4 %all-to-all-done = bf16[8,64,512]{2,1,0:T(8,128)(2,1)S(1)} async-done(((bf16[8,64,512]{2,1,0:T(8,128)(2,1)}), bf16[8,64,512]{2,1,0:T(8,128)(2,1)S(1)}, u32[]{:S(2)}, u32[]{:S(2)}) %all-to-all-start) | async-done | bytes 524320 | tf_op jit(solution)/shard_map/all_to_all | solution.py:50
  56.2 0.0 copy-start.4
  56.2 0.0 copy-done
  56.2 0.6 copy-done.4
  56.9 0.3 conditional.3
  57.1 36.2 %all_to_all.14 = bf16[8,64,512]{2,1,0:T(8,128)(2,1)S(1)} all-to-all(bf16[8,64,512]{2,1,0:T(8,128)(2,1)S(1)} %bitcast.40), channel_id=1, replica_groups=mesh['shard'=8,'rep'=4] {'shard'}, dimensions={0} | all-to-all | bytes 1048576 | tf_op jit(solution)/shard_map/all_to_all | solution.py:84
  93.3 0.4 convolution_convert_fusion.4
  93.8 0.8 copy.12
  (2 shorter events, 0.0 us)
Async XLA Ops:
  6.5 33.1 %reduce-scatter.2.cloned.1.call-start = ((), (), s32[]{:S(2)}) async-start(), calls=%async_computation.3 | async-start | bytes 1310720 | tf_op jit(solution)/shard_map/reduce_scatter | solution.py:38
  40.8 0.7 copy-start.3
  41.9 14.3 %copy-start = (bf16[1,1,2,512,512]{4,3,2,1,0:T(8,128)(2,1)S(1)}, bf16[1,1,2,512,512]{4,3,2,1,0:T(8,128)(2,1)}, u32[]{:S(2)}) copy-start(bf16[1,1,2,512,512]{4,3,2,1,0:T(8,128)(2,1)} %param.13) | copy-start | bytes 3145732
  42.8 13.4 %all-to-all-start = ((bf16[8,64,512]{2,1,0:T(8,128)(2,1)}), bf16[8,64,512]{2,1,0:T(8,128)(2,1)S(1)}, u32[]{:S(2)}, u32[]{:S(2)}) async-start(bf16[8,64,512]{2,1,0:T(8,128)(2,1)} %copy.10), calls=%async_computation.1 | async-start | bytes 1048576 | tf_op jit(solution)/shard_map/all_to_all | solution.py:50
  56.2 0.7 copy-start.4
Sparse Core Ops, SparseCore 0:
  9.6 29.9 reduce-scatter.1
where the time goes:
time: 100 us; the launch traced here: 101 us
  waiting for transfers between devices  41.5 us (42%)
  blocking collectives  36.2 us (36%)
  between operations  14.1 us (14%)
  local copies, waits for them, and re-layouts  4.18 us (4%)
  starting transfers between devices  3.66 us (4%)
    all_to_all x1, blocking collectives, local(): lax.all_to_all(update_block.reshape(shards, row_dev, block_width), 'shard...  36.2 us
    reduce_scatter x1, waiting for transfers between devices, local(): lax.psum_scatter(partial_value.astype(jnp.bfloat16), 'rep', scatter_dimen...  32.4 us
    all_to_all x1, waiting for transfers between devices, local(): lax.all_to_all(outgoing, 'shard', split_axis=0, concat_axis=1, tiled=True)  8.43 us
    all_to_all x1, starting transfers between devices, local(): lax.all_to_all(outgoing, 'shard', split_axis=0, concat_axis=1, tiled=True)  3.66 us
    unnamed x7, local copies, waits for them, and re-layouts  2.06 us
  transfers between devices with their start and end apart: 2, of which 2 were waited for; matrix products, arithmetic and copies ran while one was open for 1% of the time, Pallas kernels for 0%

commit v1 on v0

v1 whole, which is shorter than its diff:
```python
import functools

import jax
import jax.numpy as jnp
from jax import lax
from jax.experimental import pallas as pl
from jax.experimental.pallas import tpu as pltpu
from jax.sharding import PartitionSpec as P

damping = 0.1
MESH = pl.DeviceIdType.MESH
F32 = jnp.float32
BF16 = jnp.bfloat16


def dot(a, b):
    return jnp.dot(a.astype(BF16), b.astype(BF16), preferred_element_type=F32)


def total(x):
    return jnp.sum(jnp.sum(x, axis=0, keepdims=True), axis=1, keepdims=True)


def inverse_root(stat, trace):
    n = stat.shape[0]
    row = lax.broadcasted_iota(jnp.int32, (n, n), 0)
    col = lax.broadcasted_iota(jnp.int32, (n, n), 1)
    eye = row == col
    damped = stat + jnp.where(eye, damping * trace / n + 1e-06, 0.0)
    scale = 2.5 / jnp.sqrt(total(damped * damped))
    moment = damped * scale
    square = dot(moment, moment)
    q = jnp.where(eye, 25.0 / 16.0, 0.0) - 0.625 * moment + 0.0625 * square
    fm = 1.25 * moment - 0.25 * square
    qb = q.astype(BF16)
    tail = dot(dot(fm, qb), qb)
    root = jnp.where(eye, 25.0 / 16.0, 0.0) - 0.3125 * moment - 0.25 * tail
    return (root * jnp.sqrt(jnp.sqrt(scale))).astype(BF16)


def kernel(
    reps, shards, chunks,
    owner, refresh, g_hbm, roots_hbm, out,
    g, roots, rin, lin, rout, lout, acc, full, outb, gbuf, ubuf, back,
    load_sem, rs, rr, ls, lr, a_s, a_r, b_s, b_r,
):
    me = lax.axis_index("shard")
    z = lax.axis_index("rep")
    blocks, _, width = full.shape
    rows_dev = g.shape[0]
    step = rows_dev // chunks
    cols = blocks * width

    load_g = pltpu.make_async_copy(g_hbm, g, load_sem.at[0])
    load_roots = pltpu.make_async_copy(roots_hbm, roots, load_sem.at[1])
    load_g.start()
    load_roots.start()

    barrier = pltpu.get_barrier_semaphore()
    for t in range(1, shards):
        pl.semaphore_signal(
            barrier, inc=1, device_id=(lax.rem(me + t, shards), z), device_id_type=MESH
        )

    @pl.when(z > 0)
    def _():
        pl.semaphore_signal(barrier, inc=1, device_id=(me, z - 1), device_id_type=MESH)

    @pl.when(z < reps - 1)
    def _():
        pl.semaphore_signal(barrier, inc=1, device_id=(me, z + 1), device_id_type=MESH)

    peers = shards - 1 + jnp.where(z > 0, 1, 0) + jnp.where(z < reps - 1, 1, 0)
    pl.semaphore_wait(barrier, peers)

    load_g.wait()

    def rows(k):
        return pl.ds(k * step, step)

    def piece(d, k):
        return g.at[rows(k), pl.ds(pl.multiple_of(d * cols, 128), cols)]

    def right(k, dist, first):
        return pltpu.make_async_remote_copy(
            src_ref=piece(z + dist, k) if first else rout.at[k, dist - 1],
            dst_ref=rin.at[k, dist - 1],
            send_sem=rs.at[k, dist - 1],
            recv_sem=rr.at[k, dist - 1],
            device_id=(me, z + 1),
            device_id_type=MESH,
        )

    def left(k, dist, first):
        return pltpu.make_async_remote_copy(
            src_ref=piece(z - dist, k) if first else lout.at[k, dist - 1],
            dst_ref=lin.at[k, dist - 1],
            send_sem=ls.at[k, dist - 1],
            recv_sem=lr.at[k, dist - 1],
            device_id=(me, z - 1),
            device_id_type=MESH,
        )

    def arrived(buffer, sem, k, slot):
        pltpu.make_async_copy(buffer.at[k, slot], buffer.at[k, slot], sem.at[k, slot]).wait()

    @pl.when(z == 0)
    def _():
        for k in range(chunks):
            for dist in range(reps - 1, 0, -1):
                right(k, dist, True).start()

    @pl.when(z == reps - 1)
    def _():
        for k in range(chunks):
            for dist in range(reps - 1, 0, -1):
                left(k, dist, True).start()

    def slot_block(o):
        def pick(b, found):
            return jnp.where(owner[0, b] == o, b, found)

        return lax.fori_loop(0, blocks, pick, 0, unroll=blocks <= 8)

    def spread(k, t):
        return pltpu.make_async_remote_copy(
            src_ref=outb.at[k, t],
            dst_ref=gbuf.at[me, rows(k)],
            send_sem=a_s.at[k, t],
            recv_sem=a_r.at[k, t],
            device_id=(lax.rem(me + t, shards), z),
            device_id_type=MESH,
        )

    picks = [slot_block(lax.rem(me + t, shards)) for t in range(shards)]

    for k in range(chunks):
        for dist in range(reps - 2, 0, -1):

            @pl.when(jnp.logical_and(z > 0, z + dist <= reps - 1))
            def _():
                arrived(rin, rr, k, dist)
                mine = piece(z + dist, k)[...].astype(F32)
                rout[k, dist - 1] = (rin[k, dist].astype(F32) + mine).astype(BF16)
                right(k, dist, False).start()

            @pl.when(jnp.logical_and(z < reps - 1, z - dist >= 0))
            def _():
                arrived(lin, lr, k, dist)
                mine = piece(z - dist, k)[...].astype(F32)
                lout[k, dist - 1] = (lin[k, dist].astype(F32) + mine).astype(BF16)
                left(k, dist, False).start()

        acc[...] = piece(z, k)[...].astype(F32)

        @pl.when(z > 0)
        def _():
            arrived(rin, rr, k, 0)
            acc[...] += rin[k, 0].astype(F32)

        @pl.when(z < reps - 1)
        def _():
            arrived(lin, lr, k, 0)
            acc[...] += lin[k, 0].astype(F32)

        for b in range(blocks):
            full[b] = acc[:, b * width : (b + 1) * width].astype(BF16)
        for t in range(1, shards):
            outb[k, t] = full[picks[t]]
            spread(k, t).start()
        gbuf[me, k * step : (k + 1) * step] = full[picks[0]]

    load_roots.wait()
    for k in range(chunks):
        for t in range(1, shards):
            spread(k, t).wait_recv()

    size = shards * rows_dev
    if rows_dev % 16 == 0:
        grad = gbuf[...].reshape(size, width)
    else:
        grad = jnp.concatenate([gbuf[s].astype(F32) for s in range(shards)], axis=0).astype(BF16)
    values = grad.astype(F32)
    trace = total(values * values)
    mine = picks[0]
    left_new = jnp.int32(0)
    right_new = jnp.int32(0)
    for i in range(refresh.shape[1]):
        left_new += jnp.where(refresh[0, i] == 2 * mine, 1, 0)
        right_new += jnp.where(refresh[0, i] == 2 * mine + 1, 1, 0)
    left_stat = lax.dot_general(
        grad, grad, (((1,), (1,)), ((), ())), preferred_element_type=F32
    )
    right_stat = lax.dot_general(
        grad, grad, (((0,), (0,)), ((), ())), preferred_element_type=F32
    )
    new_root = inverse_root(jnp.where(right_new > 0, right_stat, left_stat), trace)
    root_left = jnp.where(left_new > 0, new_root, roots[0])
    root_right = jnp.where(right_new > 0, new_root, roots[1])
    precon = dot(dot(root_left, grad), root_right)
    count = size * width
    graft = jnp.sqrt((trace / count + 1e-06) / (total(precon * precon) / count + 1e-06))
    update = precon * graft
    if rows_dev % 16 == 0:
        ubuf[...] = update.astype(BF16).reshape(ubuf.shape)
    else:
        for s in range(shards):
            ubuf[s] = update[s * rows_dev : (s + 1) * rows_dev].astype(BF16)

    def give(t):
        return pltpu.make_async_remote_copy(
            src_ref=ubuf.at[lax.rem(me + t, shards)],
            dst_ref=back.at[me],
            send_sem=b_s.at[t],
            recv_sem=b_r.at[t],
            device_id=(lax.rem(me + t, shards), z),
            device_id_type=MESH,
        )

    for t in range(1, shards):
        give(t).start()
    back[me] = ubuf[me]
    for t in range(1, shards):
        give(t).wait_recv()
    for b in range(blocks):
        out[:, b * width : (b + 1) * width] = back[owner[0, b]]

    for t in range(1, shards):
        give(t).wait_send()
        for k in range(chunks):
            spread(k, t).wait_send()
    for k in range(chunks):
        for dist in range(1, reps):

            @pl.when(z + dist <= reps - 1)
            def _():
                right(k, dist, False).wait_send()

            @pl.when(z - dist >= 0)
            def _():
                left(k, dist, False).wait_send()


def local(grad_parts, owner_plan, refresh, roots):
    shards = lax.axis_size("shard")
    reps = lax.axis_size("rep")
    _, rows_dev, all_cols = grad_parts.shape
    width = roots.shape[-1]
    blocks = owner_plan.shape[-1]
    cols = blocks * width
    chunks = max(1, min(4, rows_dev // 16))
    step = rows_dev // chunks
    hops = max(1, reps - 1)
    dma = pltpu.SemaphoreType.DMA
    anywhere = pl.BlockSpec(memory_space=pl.ANY)
    scalars = pl.BlockSpec(memory_space=pltpu.SMEM)
    return pl.pallas_call(
        functools.partial(kernel, reps, shards, chunks),
        out_shape=jax.ShapeDtypeStruct((rows_dev, cols), BF16),
        in_specs=[scalars, scalars, anywhere, anywhere],
        out_specs=pl.BlockSpec(memory_space=pltpu.VMEM),
        scratch_shapes=[
            pltpu.VMEM((rows_dev, all_cols), BF16),
            pltpu.VMEM((2, width, width), BF16),
            pltpu.VMEM((chunks, hops, step, cols), BF16),
            pltpu.VMEM((chunks, hops, step, cols), BF16),
            pltpu.VMEM((chunks, hops, step, cols), BF16),
            pltpu.VMEM((chunks, hops, step, cols), BF16),
            pltpu.VMEM((step, cols), F32),
            pltpu.VMEM((blocks, step, width), BF16),
            pltpu.VMEM((chunks, shards, step, width), BF16),
            pltpu.VMEM((shards, rows_dev, width), BF16),
            pltpu.VMEM((shards, rows_dev, width), BF16),
            pltpu.VMEM((shards, rows_dev, width), BF16),
            dma((2,)),
            dma((chunks, hops)),
            dma((chunks, hops)),
            dma((chunks, hops)),
            dma((chunks, hops)),
            dma((chunks, shards)),
            dma((chunks, shards)),
            dma((shards,)),
            dma((shards,)),
        ],
        compiler_params=pltpu.CompilerParams(
            collective_id=0, has_side_effects=True, vmem_limit_bytes=60 * 1024 * 1024
        ),
    )(owner_plan, refresh, grad_parts[0], roots[0, 0])


def solution(mesh):
    placed = (
        P("rep", "shard", None),
        P("rep", None),
        P("rep", None),
        P("rep", "shard", None, None, None),
    )
    return jax.shard_map(
        local, mesh=mesh, in_specs=placed, out_specs=P("shard", "rep"), check_vma=False
    )
```

time: 100 us -> 51.1 us (0.51); the launches traced: 101 us -> 50.2 us
  Pallas kernels: 0 us -> 48.6 us
  waiting for transfers between devices: 41.5 us -> 0 us
  blocking collectives: 36.2 us -> 0 us
  between operations: 14.1 us -> 0.01 us
  starting transfers between devices: 3.66 us -> 0 us
  local copies, waits for them, and re-layouts: 4.18 us -> 1.67 us
    pallas_call x0 -> x1, Pallas kernels: none -> 48.6 us  [local(): pl.pallas_call(functools.partial(kernel, reps, shards, chunks), out_shape...]
    all_to_all x1 -> x0, blocking collectives: 36.2 us -> none  [local(): lax.all_to_all(update_block.reshape(shards, row_dev, block_width), 'shard...]
    reduce_scatter x1 -> x0, waiting for transfers between devices: 32.4 us -> none  [local(): lax.psum_scatter(partial_value.astype(jnp.bfloat16), 'rep', scatter_dimen...]
    all_to_all x1 -> x0, waiting for transfers between devices: 8.43 us -> none  [local(): lax.all_to_all(outgoing, 'shard', split_axis=0, concat_axis=1, tiled=True)]
    all_to_all x1 -> x0, starting transfers between devices: 3.66 us -> none  [local(): lax.all_to_all(outgoing, 'shard', split_axis=0, concat_axis=1, tiled=True)]
    reshape x1 -> x0, local copies, waits for them, and re-layouts: 1.13 us -> none  [local(): pieces = my_columns.reshape(row_dev, block_count, block_width)]
    unnamed x7 -> x1, local copies, waits for them, and re-layouts: 2.06 us -> 1.67 us
  transfers between devices with their start and end apart: 2 -> 0, of which waited for: 2 -> 0; matrix products, arithmetic and copies ran while one was open for 1% -> 0% of each run, Pallas kernels for 0% -> 0%
where the time goes in v1:
time: 51.1 us; the launch traced here: 50.2 us
  Pallas kernels  48.6 us (95%)
  local copies, waits for them, and re-layouts  1.67 us (3%)
    pallas_call x1, Pallas kernels, local(): pl.pallas_call(functools.partial(kernel, reps, shards, chunks), out_shape...  48.6 us
    unnamed x1, local copies, waits for them, and re-layouts  1.67 us

profile of v1, /device:TPU:0, one launch (start us, length us, event | category | flops | bytes accessed | tf_op | source)
XLA Modules:
  0.0 50.2 jit_solution(5685185927852747567)
XLA Ops:
  0.0 48.6 %shard_map.46 = bf16[64,2048]{1,0:T(8,128)(2,1)} custom-call(s32[1,4]{1,0:T(1,128)} %owner.1, s32[1,2]{1,0:T(1,128)} %refresh.1, bf16[64,8192]{1,0:T(8,128)(2,1)} %bitcast.2, bf16[2,512,512]{2,1,0:T(8,128)(2,1)} %bitcast.3), custom_call_target="tpu_custom_call" | custom-call | tf_op jit(solution)/shard_map/pallas_call | solution.py:257
  48.6 1.7 %copy.6 = bf16[64,2048]{1,0:T(8,128)(2,1)} copy(bf16[64,2048]{1,0:T(8,128)(2,1)} %shard_map.46) | data formatting | bytes 524288

commit v2 on v1

--- a/solution.py
+++ b/solution.py
@@ -106,14 +106,14 @@
 
     @pl.when(z == 0)
     def _():
-        for k in range(chunks):
-            for dist in range(reps - 1, 0, -1):
+        for dist in range(reps - 1, 0, -1):
+            for k in range(chunks):
                 right(k, dist, True).start()
 
     @pl.when(z == reps - 1)
     def _():
-        for k in range(chunks):
-            for dist in range(reps - 1, 0, -1):
+        for dist in range(reps - 1, 0, -1):
+            for k in range(chunks):
                 left(k, dist, True).start()
 
     def slot_block(o):
@@ -134,8 +134,8 @@
 
     picks = [slot_block(lax.rem(me + t, shards)) for t in range(shards)]
 
-    for k in range(chunks):
-        for dist in range(reps - 2, 0, -1):
+    for dist in range(reps - 2, 0, -1):
+        for k in range(chunks):
 
             @pl.when(jnp.logical_and(z > 0, z + dist <= reps - 1))
             def _():
@@ -151,6 +151,7 @@
                 lout[k, dist - 1] = (lin[k, dist].astype(F32) + mine).astype(BF16)
                 left(k, dist, False).start()
 
+    for k in range(chunks):
         acc[...] = piece(z, k)[...].astype(F32)
 
         @pl.when(z > 0)

time: 51.1 us -> 40.1 us (0.78)
  the two profiles are of different devices: /device:TPU:0 before, /device:TPU:17 now
where the time goes in v2:
time: 40.1 us; the launch traced here: 40 us
  Pallas kernels  38.3 us (96%)
  local copies, waits for them, and re-layouts  1.67 us (4%)
    pallas_call x1, Pallas kernels, local(): pl.pallas_call(functools.partial(kernel, reps, shards, chunks), out_shape...  38.3 us
    unnamed x1, local copies, waits for them, and re-layouts  1.67 us

profile of v2, /device:TPU:17, one launch (start us, length us, event | category | flops | bytes accessed | tf_op | source)
XLA Modules:
  0.0 40.0 jit_solution(6931899956622421123)
XLA Ops:
  0.0 38.3 %shard_map.46 = bf16[64,2048]{1,0:T(8,128)(2,1)} custom-call(s32[1,4]{1,0:T(1,128)} %owner.1, s32[1,2]{1,0:T(1,128)} %refresh.1, bf16[64,8192]{1,0:T(8,128)(2,1)} %bitcast.2, bf16[2,512,512]{2,1,0:T(8,128)(2,1)} %bitcast.3), custom_call_target="tpu_custom_call" | custom-call | tf_op jit(solution)/shard_map/pallas_call | solution.py:258
  38.3 1.7 %copy.6 = bf16[64,2048]{1,0:T(8,128)(2,1)} copy(bf16[64,2048]{1,0:T(8,128)(2,1)} %shard_map.46) | data formatting | bytes 524288

commit v3 on v2

v3 whole, which is shorter than its diff:
```python
import functools

import jax
import jax.numpy as jnp
from jax import lax
from jax.experimental import pallas as pl
from jax.experimental.pallas import tpu as pltpu
from jax.sharding import PartitionSpec as P

damping = 0.1
MESH = pl.DeviceIdType.MESH
F32 = jnp.float32
BF16 = jnp.bfloat16


def dot(a, b):
    return jnp.dot(a.astype(BF16), b.astype(BF16), preferred_element_type=F32)


def total(x):
    return jnp.sum(jnp.sum(x, axis=0, keepdims=True), axis=1, keepdims=True)


def inverse_root(stat, trace):
    n = stat.shape[0]
    row = lax.broadcasted_iota(jnp.int32, (n, n), 0)
    col = lax.broadcasted_iota(jnp.int32, (n, n), 1)
    eye = row == col
    damped = stat + jnp.where(eye, damping * trace / n + 1e-06, 0.0)
    scale = 2.5 / jnp.sqrt(total(damped * damped))
    moment = damped * scale
    square = dot(moment, moment)
    q = jnp.where(eye, 25.0 / 16.0, 0.0) - 0.625 * moment + 0.0625 * square
    fm = 1.25 * moment - 0.25 * square
    qb = q.astype(BF16)
    tail = dot(dot(fm, qb), qb)
    root = jnp.where(eye, 25.0 / 16.0, 0.0) - 0.3125 * moment - 0.25 * tail
    return (root * jnp.sqrt(jnp.sqrt(scale))).astype(BF16)


def mix(a, t, n):
    if n & (n - 1):
        return lax.rem(a + t, n)
    out, bit = a, 1
    while bit < n:
        if t & bit:
            out = out + bit - 2 * bit * lax.rem(a // bit, 2)
        bit *= 2
    return out


def unmix(a, t, n):
    return lax.rem(a + n - t, n) if n & (n - 1) else mix(a, t, n)


def whole_block(ref, rows_dev):
    shards, _, width = ref.shape
    if rows_dev % 16 == 0:
        return ref[...].reshape(shards * rows_dev, width)
    return jnp.concatenate([ref[s].astype(F32) for s in range(shards)], axis=0).astype(BF16)


def precondition(shards, rows_dev, refresh, mine, gbuf, roots, ubuf, landed_roots):
    grad = whole_block(gbuf, rows_dev)
    size, width = grad.shape
    values = grad.astype(F32)
    trace = total(values * values)
    left_new = jnp.int32(0)
    right_new = jnp.int32(0)
    for i in range(refresh.shape[1]):
        left_new += jnp.where(refresh[0, i] == 2 * mine, 1, 0)
        right_new += jnp.where(refresh[0, i] == 2 * mine + 1, 1, 0)
    left_stat = lax.dot_general(
        grad, grad, (((1,), (1,)), ((), ())), preferred_element_type=F32
    )
    right_stat = lax.dot_general(
        grad, grad, (((0,), (0,)), ((), ())), preferred_element_type=F32
    )
    new_root = inverse_root(jnp.where(right_new > 0, right_stat, left_stat), trace)
    landed_roots()
    root_left = jnp.where(left_new > 0, new_root, whole_block(roots.at[0], rows_dev))
    root_right = jnp.where(right_new > 0, new_root, whole_block(roots.at[1], rows_dev))
    precon = dot(dot(root_left, grad), root_right)
    count = size * width
    graft = jnp.sqrt((trace / count + 1e-06) / (total(precon * precon) / count + 1e-06))
    update = precon * graft
    if rows_dev % 16 == 0:
        ubuf[...] = update.astype(BF16).reshape(ubuf.shape)
    else:
        for s in range(shards):
            ubuf[s] = update[s * rows_dev : (s + 1) * rows_dev].astype(BF16)


def kernel(
    reps, shards, chunks,
    owner, refresh, g_hbm, roots_hbm, out,
    g, rin, lin, rout, lout, acc, full, gbuf, ubuf, slices, chosen, roots,
    load_sem, rs, rr, ls, lr, a_s, a_r, b_s, b_r, c_s, c_r, d_s, d_r,
):
    me = lax.axis_index("shard")
    z = lax.axis_index("rep")
    _, blocks, step, width = full.shape
    rows_dev = g.shape[0]
    cols = blocks * width
    per = shards // blocks
    mine = me // per
    is_home = lax.rem(me, per) == 0
    not_home = lax.rem(me, per) > 0

    load_g = pltpu.make_async_copy(g_hbm, g, load_sem.at[0])
    load_g.start()
    keep = pltpu.make_async_copy(
        roots_hbm.at[:, pl.ds(pl.multiple_of(me * rows_dev, 8), rows_dev)],
        slices.at[me],
        load_sem.at[1],
    )
    keep.start()

    barrier = pltpu.get_barrier_semaphore()
    for t in range(1, shards):
        pl.semaphore_signal(
            barrier, inc=1, device_id=(lax.rem(me + t, shards), z), device_id_type=MESH
        )

    @pl.when(z > 0)
    def _():
        pl.semaphore_signal(barrier, inc=1, device_id=(me, z - 1), device_id_type=MESH)

    @pl.when(z < reps - 1)
    def _():
        pl.semaphore_signal(barrier, inc=1, device_id=(me, z + 1), device_id_type=MESH)

    peers = shards - 1 + jnp.where(z > 0, 1, 0) + jnp.where(z < reps - 1, 1, 0)
    pl.semaphore_wait(barrier, peers)

    def cut(t):
        peer = mix(me, t, shards)
        return pltpu.make_async_remote_copy(
            src_ref=roots_hbm.at[:, pl.ds(pl.multiple_of(peer * rows_dev, 8), rows_dev)],
            dst_ref=slices.at[me],
            send_sem=c_s.at[t],
            recv_sem=c_r.at[me],
            device_id=(peer, z),
            device_id_type=MESH,
        )

    load_g.wait()

    def rows(k):
        return pl.ds(k * step, step)

    def piece(d, k):
        return g.at[rows(k), pl.ds(pl.multiple_of(d * cols, 128), cols)]

    def right(k, dist, first):
        return pltpu.make_async_remote_copy(
            src_ref=piece(z + dist, k) if first else rout.at[k, dist - 1],
            dst_ref=rin.at[k, dist - 1],
            send_sem=rs.at[k, dist - 1],
            recv_sem=rr.at[k, dist - 1],
            device_id=(me, z + 1),
            device_id_type=MESH,
        )

    def left(k, dist, first):
        return pltpu.make_async_remote_copy(
            src_ref=piece(z - dist, k) if first else lout.at[k, dist - 1],
            dst_ref=lin.at[k, dist - 1],
            send_sem=ls.at[k, dist - 1],
            recv_sem=lr.at[k, dist - 1],
            device_id=(me, z - 1),
            device_id_type=MESH,
        )

    def arrived(buffer, sem, k, slot):
        pltpu.make_async_copy(buffer.at[k, slot], buffer.at[k, slot], sem.at[k, slot]).wait()

    @pl.when(z == 0)
    def _():
        for dist in range(reps - 1, 0, -1):
            for k in range(chunks):
                right(k, dist, True).start()

    @pl.when(z == reps - 1)
    def _():
        for dist in range(reps - 1, 0, -1):
            for k in range(chunks):
                left(k, dist, True).start()

    for t in range(shards - 1, 0, -1):
        cut(t).start()

    def to_home(j, src, dst, send, recv):
        return pltpu.make_async_remote_copy(
            src_ref=src,
            dst_ref=dst,
            send_sem=send,
            recv_sem=recv,
            device_id=(mix(mine, j, blocks) * per, z),
            device_id_type=MESH,
        )

    def lend(j):
        return to_home(j, chosen.at[j], roots.at[:, me], d_s.at[j], d_r.at[me])

    def spread(k, j):
        b = mix(mine, j, blocks)
        return to_home(j, full.at[k, b], gbuf.at[me, rows(k)], a_s.at[k, j], a_r.at[k, me])

    def landed(ref, sem):
        pltpu.make_async_copy(ref, ref, sem).wait()

    for dist in range(reps - 2, 0, -1):
        for k in range(chunks):

            @pl.when(jnp.logical_and(z > 0, z + dist <= reps - 1))
            def _():
                arrived(rin, rr, k, dist)
                mine = piece(z + dist, k)[...].astype(F32)
                rout[k, dist - 1] = (rin[k, dist].astype(F32) + mine).astype(BF16)
                right(k, dist, False).start()

            @pl.when(jnp.logical_and(z < reps - 1, z - dist >= 0))
            def _():
                arrived(lin, lr, k, dist)
                mine = piece(z - dist, k)[...].astype(F32)
                lout[k, dist - 1] = (lin[k, dist].astype(F32) + mine).astype(BF16)
                left(k, dist, False).start()

    keep.wait()
    for t in range(shards - 1, 0, -1):
        peer = unmix(me, t, shards)
        landed(slices.at[peer], c_r.at[peer])
    for j in range(blocks - 1, 0, -1):
        chosen[j] = slices[owner[0, mix(mine, j, blocks)]]
        lend(j).start()

    @pl.when(is_home)
    def _():
        roots[:, me] = slices[owner[0, mine]]

    @pl.when(not_home)
    def _():
        chosen[0] = slices[owner[0, mine]]
        lend(0).start()

    for k in range(chunks):
        acc[...] = piece(z, k)[...].astype(F32)

        @pl.when(z > 0)
        def _():
            arrived(rin, rr, k, 0)
            acc[...] += rin[k, 0].astype(F32)

        @pl.when(z < reps - 1)
        def _():
            arrived(lin, lr, k, 0)
            acc[...] += lin[k, 0].astype(F32)

        for b in range(blocks):
            full[k, b] = acc[:, b * width : (b + 1) * width].astype(BF16)
        for j in range(blocks - 1, 0, -1):
            spread(k, j).start()

        @pl.when(is_home)
        def _():
            gbuf[me, k * step : (k + 1) * step] = full[k, mine]

        @pl.when(not_home)
        def _():
            spread(k, 0).start()

    def give(t):
        peer = mix(me, t, shards)
        return pltpu.make_async_remote_copy(
            src_ref=ubuf.at[peer],
            dst_ref=place(mine),
            send_sem=b_s.at[t],
            recv_sem=b_r.at[mine],
            device_id=(peer, z),
            device_id_type=MESH,
        )

    def place(b):
        return out.at[:, pl.ds(pl.multiple_of(b * width, 128), width)]

    def landed_roots():
        for t in range(shards - 1, 0, -1):
            peer = unmix(me, t, shards)
            landed(roots.at[:, peer], d_r.at[peer])

    put = pltpu.make_async_copy(ubuf.at[me], place(mine), load_sem.at[2])

    @pl.when(is_home)
    def _():
        for k in range(chunks):
            for t in range(shards - 1, 0, -1):
                peer = unmix(me, t, shards)
                landed(gbuf.at[peer, rows(k)], a_r.at[k, peer])
        precondition(shards, rows_dev, refresh, mine, gbuf, roots, ubuf, landed_roots)
        for t in range(shards - 1, 0, -1):
            give(t).start()
        put.start()

    for j in range(blocks - 1, 0, -1):
        b = unmix(mine, j, blocks)
        landed(place(b), b_r.at[b])

    @pl.when(not_home)
    def _():
        landed(place(mine), b_r.at[mine])
        lend(0).wait_send()
        for k in range(chunks):
            spread(k, 0).wait_send()

    @pl.when(is_home)
    def _():
        put.wait()
        for t in range(1, shards):
            give(t).wait_send()

    for t in range(1, shards):
        cut(t).wait_send()
    for j in range(1, blocks):
        lend(j).wait_send()
        for k in range(chunks):
            spread(k, j).wait_send()
    for k in range(chunks):
        for dist in range(1, reps):

            @pl.when(z + dist <= reps - 1)
            def _():
                right(k, dist, False).wait_send()

            @pl.when(z - dist >= 0)
            def _():
                left(k, dist, False).wait_send()


def local(grad_parts, owner_plan, refresh, roots):
    shards = lax.axis_size("shard")
    reps = lax.axis_size("rep")
    _, rows_dev, all_cols = grad_parts.shape
    width = roots.shape[-1]
    blocks = owner_plan.shape[-1]
    cols = blocks * width
    chunks = max(1, min(4, rows_dev // 16))
    step = rows_dev // chunks
    hops = max(1, reps - 1)
    dma = pltpu.SemaphoreType.DMA
    anywhere = pl.BlockSpec(memory_space=pl.ANY)
    scalars = pl.BlockSpec(memory_space=pltpu.SMEM)
    return pl.pallas_call(
        functools.partial(kernel, reps, shards, chunks),
        out_shape=jax.ShapeDtypeStruct((rows_dev, cols), BF16),
        in_specs=[scalars, scalars, anywhere, anywhere],
        out_specs=anywhere,
        scratch_shapes=[
            pltpu.VMEM((rows_dev, all_cols), BF16),
            pltpu.VMEM((chunks, hops, step, cols), BF16),
            pltpu.VMEM((chunks, hops, step, cols), BF16),
            pltpu.VMEM((chunks, hops, step, cols), BF16),
            pltpu.VMEM((chunks, hops, step, cols), BF16),
            pltpu.VMEM((step, cols), F32),
            pltpu.VMEM((chunks, blocks, step, width), BF16),
            pltpu.VMEM((shards, rows_dev, width), BF16),
            pltpu.VMEM((shards, rows_dev, width), BF16),
            pltpu.VMEM((shards, 2, rows_dev, width), BF16),
            pltpu.VMEM((blocks, 2, rows_dev, width), BF16),
            pltpu.VMEM((2, shards, rows_dev, width), BF16),
            dma((3,)),
            dma((chunks, hops)),
            dma((chunks, hops)),
            dma((chunks, hops)),
            dma((chunks, hops)),
            dma((chunks, blocks)),
            dma((chunks, shards)),
            dma((shards,)),
            dma((blocks,)),
            dma((shards,)),
            dma((shards,)),
            dma((blocks,)),
            dma((shards,)),
        ],
        compiler_params=pltpu.CompilerParams(
            collective_id=0, has_side_effects=True, vmem_limit_bytes=60 * 1024 * 1024
        ),
    )(owner_plan, refresh, grad_parts[0], roots[0, 0])


def solution(mesh):
    placed = (
        P("rep", "shard", None),
        P("rep", None),
        P("rep", None),
        P("rep", "shard", None, None, None),
    )
    return jax.shard_map(
        local, mesh=mesh, in_specs=placed, out_specs=P("shard", "rep"), check_vma=False
    )
```

time: 40.1 us -> 40.3 us (level)
  the two profiles are of different devices: /device:TPU:17 before, /device:TPU:0 now
where the time goes in v3:
time: 40.3 us; the launch traced here: 40.1 us
  Pallas kernels  38.5 us (96%)
  local copies, waits for them, and re-layouts  1.67 us (4%)
    pallas_call x1, Pallas kernels, local(): pl.pallas_call(functools.partial(kernel, reps, shards, chunks), out_shape...  38.5 us
    unnamed x1, local copies, waits for them, and re-layouts  1.67 us

profile of v3, /device:TPU:0, one launch (start us, length us, event | category | flops | bytes accessed | tf_op | source)
XLA Modules:
  0.0 40.1 jit_solution(397959214744457726)
XLA Ops:
  0.0 38.5 %shard_map.46 = bf16[64,2048]{1,0:T(8,128)(2,1)} custom-call(s32[1,4]{1,0:T(1,128)} %owner.1, s32[1,2]{1,0:T(1,128)} %refresh.1, bf16[64,8192]{1,0:T(8,128)(2,1)} %bitcast.2, bf16[2,512,512]{2,1,0:T(8,128)(2,1)} %bitcast.3), custom_call_target="tpu_custom_call" | custom-call | tf_op jit(solution)/shard_map/pallas_call | solution.py:353
  38.5 1.7 %copy.6 = bf16[64,2048]{1,0:T(8,128)(2,1)} copy(bf16[64,2048]{1,0:T(8,128)(2,1)} %shard_map.46) | data formatting | bytes 524288

commit v4 on v3

--- a/solution.py
+++ b/solution.py
@@ -94,7 +94,7 @@
 def kernel(
     reps, shards, chunks,
     owner, refresh, g_hbm, roots_hbm, out,
-    g, rin, lin, rout, lout, acc, full, gbuf, ubuf, slices, chosen, roots,
+    g, rin, lin, rout, lout, acc, full, gbuf, ubuf, left_cuts, right_cuts, chosen, roots,
     load_sem, rs, rr, ls, lr, a_s, a_r, b_s, b_r, c_s, c_r, d_s, d_r,
 ):
     me = lax.axis_index("shard")
@@ -109,12 +109,17 @@
 
     load_g = pltpu.make_async_copy(g_hbm, g, load_sem.at[0])
     load_g.start()
-    keep = pltpu.make_async_copy(
-        roots_hbm.at[:, pl.ds(pl.multiple_of(me * rows_dev, 8), rows_dev)],
-        slices.at[me],
-        load_sem.at[1],
-    )
-    keep.start()
+    slices = (left_cuts, right_cuts)
+    keep = [
+        pltpu.make_async_copy(
+            roots_hbm.at[i, pl.ds(pl.multiple_of(me * rows_dev, 8), rows_dev)],
+            slices[i].at[me],
+            load_sem.at[1 + i],
+        )
+        for i in range(2)
+    ]
+    for copy in keep:
+        copy.start()
 
     barrier = pltpu.get_barrier_semaphore()
     for t in range(1, shards):
@@ -133,13 +138,13 @@
     peers = shards - 1 + jnp.where(z > 0, 1, 0) + jnp.where(z < reps - 1, 1, 0)
     pl.semaphore_wait(barrier, peers)
 
-    def cut(t):
+    def cut(i, t):
         peer = mix(me, t, shards)
         return pltpu.make_async_remote_copy(
-            src_ref=roots_hbm.at[:, pl.ds(pl.multiple_of(peer * rows_dev, 8), rows_dev)],
-            dst_ref=slices.at[me],
-            send_sem=c_s.at[t],
-            recv_sem=c_r.at[me],
+            src_ref=roots_hbm.at[i, pl.ds(pl.multiple_of(peer * rows_dev, 8), rows_dev)],
+            dst_ref=slices[i].at[me],
+            send_sem=c_s.at[i, t],
+            recv_sem=c_r.at[i, me],
             device_id=(peer, z),
             device_id_type=MESH,
         )
@@ -187,8 +192,9 @@
             for k in range(chunks):
                 left(k, dist, True).start()
 
-    for t in range(shards - 1, 0, -1):
-        cut(t).start()
+    for i in range(2):
+        for t in range(shards - 1, 0, -1):
+            cut(i, t).start()
 
     def to_home(j, src, dst, send, recv):
         return pltpu.make_async_remote_copy(
@@ -200,8 +206,8 @@
             device_id_type=MESH,
         )
 
-    def lend(j):
-        return to_home(j, chosen.at[j], roots.at[:, me], d_s.at[j], d_r.at[me])
+    def lend(i, j):
+        return to_home(j, chosen.at[i, j], roots.at[i, me], d_s.at[i, j], d_r.at[i, me])
 
     def spread(k, j):
         b = mix(mine, j, blocks)
@@ -210,7 +216,28 @@
     def landed(ref, sem):
         pltpu.make_async_copy(ref, ref, sem).wait()
 
+    def pass_on(i):
+        for t in range(shards - 1, 0, -1):
+            peer = unmix(me, t, shards)
+            landed(slices[i].at[peer], c_r.at[i, peer])
+        for j in range(blocks - 1, 0, -1):
+            chosen[i, j] = slices[i][owner[0, mix(mine, j, blocks)]]
+            lend(i, j).start()
+
+        @pl.when(is_home)
+        def _():
+            roots[i, me] = slices[i][owner[0, mine]]
+
+        @pl.when(not_home)
+        def _():
+            chosen[i, 0] = slices[i][owner[0, mine]]
+            lend(i, 0).start()
+
+    for copy in keep:
+        copy.wait()
     for dist in range(reps - 2, 0, -1):
+        if dist == 1:
+            pass_on(0)
         for k in range(chunks):
 
             @pl.when(jnp.logical_and(z > 0, z + dist <= reps - 1))
@@ -227,22 +254,8 @@
                 lout[k, dist - 1] = (lin[k, dist].astype(F32) + mine).astype(BF16)
                 left(k, dist, False).start()
 
-    keep.wait()
-    for t in range(shards - 1, 0, -1):
-        peer = unmix(me, t, shards)
-        landed(slices.at[peer], c_r.at[peer])
-    for j in range(blocks - 1, 0, -1):
-        chosen[j] = slices[owner[0, mix(mine, j, blocks)]]
-        lend(j).start()
-
-    @pl.when(is_home)
-    def _():
-        roots[:, me] = slices[owner[0, mine]]
-
-    @pl.when(not_home)
-    def _():
-        chosen[0] = slices[owner[0, mine]]
-        lend(0).start()
+    for i in range(1 if reps > 2 else 0, 2):
+        pass_on(i)
 
     for k in range(chunks):
         acc[...] = piece(z, k)[...].astype(F32)
@@ -285,11 +298,12 @@
         return out.at[:, pl.ds(pl.multiple_of(b * width, 128), width)]
 
     def landed_roots():
-        for t in range(shards - 1, 0, -1):
-            peer = unmix(me, t, shards)
-            landed(roots.at[:, peer], d_r.at[peer])
-
-    put = pltpu.make_async_copy(ubuf.at[me], place(mine), load_sem.at[2])
+        for i in range(2):
+            for t in range(shards - 1, 0, -1):
+                peer = unmix(me, t, shards)
+                landed(roots.at[i, peer], d_r.at[i, peer])
+
+    put = pltpu.make_async_copy(ubuf.at[me], place(mine), load_sem.at[3])
 
     @pl.when(is_home)
     def _():
@@ -309,7 +323,8 @@
     @pl.when(not_home)
     def _():
         landed(place(mine), b_r.at[mine])
-        lend(0).wait_send()
+        for i in range(2):
+            lend(i, 0).wait_send()
         for k in range(chunks):
             spread(k, 0).wait_send()
 
@@ -320,9 +335,11 @@
             give(t).wait_send()
 
     for t in range(1, shards):
-        cut(t).wait_send()
+        for i in range(2):
+            cut(i, t).wait_send()
     for j in range(1, blocks):
-        lend(j).wait_send()
+        for i in range(2):
+            lend(i, j).wait_send()
         for k in range(chunks):
             spread(k, j).wait_send()
     for k in range(chunks):
@@ -344,7 +361,7 @@
     width = roots.shape[-1]
     blocks = owner_plan.shape[-1]
     cols = blocks * width
-    chunks = max(1, min(4, rows_dev // 16))
+    chunks = max(1, min(2, rows_dev // 16))
     step = rows_dev // chunks
     hops = max(1, reps - 1)
     dma = pltpu.SemaphoreType.DMA
@@ -365,10 +382,11 @@
             pltpu.VMEM((chunks, blocks, step, width), BF16),
             pltpu.VMEM((shards, rows_dev, width), BF16),
             pltpu.VMEM((shards, rows_dev, width), BF16),
-            pltpu.VMEM((shards, 2, rows_dev, width), BF16),
-            pltpu.VMEM((blocks, 2, rows_dev, width), BF16),
+            pltpu.VMEM((shards, rows_dev, width), BF16),
+            pltpu.VMEM((shards, rows_dev, width), BF16),
+            pltpu.VMEM((2, blocks, rows_dev, width), BF16),
             pltpu.VMEM((2, shards, rows_dev, width), BF16),
-            dma((3,)),
+            dma((4,)),
             dma((chunks, hops)),
             dma((chunks, hops)),
             dma((chunks, hops)),
@@ -377,10 +395,10 @@
             dma((chunks, shards)),
             dma((shards,)),
             dma((blocks,)),
-            dma((shards,)),
-            dma((shards,)),
-            dma((blocks,)),
-            dma((shards,)),
+            dma((2, shards)),
+            dma((2, shards)),
+            dma((2, blocks)),
+            dma((2, shards)),
         ],
         compiler_params=pltpu.CompilerParams(
             collective_id=0, has_side_effects=True, vmem_limit_bytes=60 * 1024 * 1024

time: 40.3 us -> 38 us (0.943)
  Pallas kernels: 38.5 us -> 36.2 us
    pallas_call x1, Pallas kernels: 38.5 us -> 36.2 us  [local(): pl.pallas_call(functools.partial(kernel, reps, shards, chunks), out_shape...]
where the time goes in v4:
time: 38 us; the launch traced here: 37.9 us
  Pallas kernels  36.2 us (95%)
  local copies, waits for them, and re-layouts  1.67 us (4%)
    pallas_call x1, Pallas kernels, local(): pl.pallas_call(functools.partial(kernel, reps, shards, chunks), out_shape...  36.2 us
    unnamed x1, local copies, waits for them, and re-layouts  1.67 us

profile of v4, /device:TPU:0, one launch (start us, length us, event | category | flops | bytes accessed | tf_op | source)
XLA Modules:
  0.0 37.9 jit_solution(5353024512737968353)
XLA Ops:
  0.0 36.2 %shard_map.46 = bf16[64,2048]{1,0:T(8,128)(2,1)} custom-call(s32[1,4]{1,0:T(1,128)} %owner.1, s32[1,2]{1,0:T(1,128)} %refresh.1, bf16[64,8192]{1,0:T(8,128)(2,1)} %bitcast.2, bf16[2,512,512]{2,1,0:T(8,128)(2,1)} %bitcast.3), custom_call_target="tpu_custom_call" | custom-call | tf_op jit(solution)/shard_map/pallas_call | solution.py:370
  36.2 1.7 %copy.6 = bf16[64,2048]{1,0:T(8,128)(2,1)} copy(bf16[64,2048]{1,0:T(8,128)(2,1)} %shard_map.46) | data formatting | bytes 524288

commit v5 on v4

--- a/solution.py
+++ b/solution.py
@@ -60,7 +60,7 @@
     return jnp.concatenate([ref[s].astype(F32) for s in range(shards)], axis=0).astype(BF16)
 
 
-def precondition(shards, rows_dev, refresh, mine, gbuf, roots, ubuf, landed_roots):
+def precondition(shards, rows_dev, refresh, mine, gbuf, roots, ubuf, landed_roots, gscale, send_rows):
     grad = whole_block(gbuf, rows_dev)
     size, width = grad.shape
     values = grad.astype(F32)
@@ -80,22 +80,30 @@
     landed_roots()
     root_left = jnp.where(left_new > 0, new_root, whole_block(roots.at[0], rows_dev))
     root_right = jnp.where(right_new > 0, new_root, whole_block(roots.at[1], rows_dev))
-    precon = dot(dot(root_left, grad), root_right)
+    left_part = dot(root_left, grad).astype(BF16)
     count = size * width
-    graft = jnp.sqrt((trace / count + 1e-06) / (total(precon * precon) / count + 1e-06))
-    update = precon * graft
-    if rows_dev % 16 == 0:
-        ubuf[...] = update.astype(BF16).reshape(ubuf.shape)
-    else:
-        for s in range(shards):
-            ubuf[s] = update[s * rows_dev : (s + 1) * rows_dev].astype(BF16)
+    squares = jnp.zeros((1, 1), F32)
+    group = max(1, shards // 4)
+    for start in range(0, shards, group):
+        span = group * rows_dev
+        precon = dot(left_part[start * rows_dev : start * rows_dev + span], root_right)
+        squares += total(precon * precon)
+        if rows_dev % 16 == 0:
+            ubuf[start : start + group] = precon.astype(BF16).reshape(group, rows_dev, width)
+        else:
+            for s in range(group):
+                ubuf[start + s] = precon[s * rows_dev : (s + 1) * rows_dev].astype(BF16)
+        for s in range(start, start + group):
+            send_rows(s)
+    graft = jnp.sqrt((trace / count + 1e-06) / (squares / count + 1e-06))
+    gscale[...] = jnp.broadcast_to(graft, gscale.shape)
 
 
 def kernel(
     reps, shards, chunks,
-    owner, refresh, g_hbm, roots_hbm, out,
-    g, rin, lin, rout, lout, acc, full, gbuf, ubuf, left_cuts, right_cuts, chosen, roots,
-    load_sem, rs, rr, ls, lr, a_s, a_r, b_s, b_r, c_s, c_r, d_s, d_r,
+    owner, refresh, g_hbm, roots_hbm, out, scales,
+    g, rin, lin, rout, lout, acc, full, gbuf, ubuf, left_cuts, right_cuts, chosen, roots, gscale,
+    load_sem, rs, rr, ls, lr, a_s, a_r, b_s, b_r, e_s, e_r, c_s, c_r, d_s, d_r,
 ):
     me = lax.axis_index("shard")
     z = lax.axis_index("rep")
@@ -283,16 +291,34 @@
         def _():
             spread(k, 0).start()
 
-    def give(t):
-        peer = mix(me, t, shards)
+    def give(peer):
         return pltpu.make_async_remote_copy(
             src_ref=ubuf.at[peer],
             dst_ref=place(mine),
-            send_sem=b_s.at[t],
+            send_sem=b_s.at[peer],
             recv_sem=b_r.at[mine],
             device_id=(peer, z),
             device_id_type=MESH,
         )
+
+    def give_scale(t):
+        peer = mix(me, t, shards)
+        return pltpu.make_async_remote_copy(
+            src_ref=gscale,
+            dst_ref=scale_place(mine),
+            send_sem=e_s.at[t],
+            recv_sem=e_r.at[mine],
+            device_id=(peer, z),
+            device_id_type=MESH,
+        )
+
+    def scale_place(b):
+        return scales.at[:, pl.ds(pl.multiple_of(b * width, 128), width)]
+
+    def send_rows(s):
+        @pl.when(me != s)
+        def _():
+            give(s).start()
 
     def place(b):
         return out.at[:, pl.ds(pl.multiple_of(b * width, 128), width)]
@@ -303,6 +329,7 @@
                 peer = unmix(me, t, shards)
                 landed(roots.at[i, peer], d_r.at[i, peer])
 
+    put_scale = pltpu.make_async_copy(gscale, scale_place(mine), load_sem.at[4])
     put = pltpu.make_async_copy(ubuf.at[me], place(mine), load_sem.at[3])
 
     @pl.when(is_home)
@@ -311,18 +338,21 @@
             for t in range(shards - 1, 0, -1):
                 peer = unmix(me, t, shards)
                 landed(gbuf.at[peer, rows(k)], a_r.at[k, peer])
-        precondition(shards, rows_dev, refresh, mine, gbuf, roots, ubuf, landed_roots)
+        precondition(shards, rows_dev, refresh, mine, gbuf, roots, ubuf, landed_roots, gscale, send_rows)
         for t in range(shards - 1, 0, -1):
-            give(t).start()
+            give_scale(t).start()
         put.start()
+        put_scale.start()
 
     for j in range(blocks - 1, 0, -1):
         b = unmix(mine, j, blocks)
         landed(place(b), b_r.at[b])
+        landed(scale_place(b), e_r.at[b])
 
     @pl.when(not_home)
     def _():
         landed(place(mine), b_r.at[mine])
+        landed(scale_place(mine), e_r.at[mine])
         for i in range(2):
             lend(i, 0).wait_send()
         for k in range(chunks):
@@ -331,8 +361,10 @@
     @pl.when(is_home)
     def _():
         put.wait()
+        put_scale.wait()
         for t in range(1, shards):
-            give(t).wait_send()
+            give(mix(me, t, shards)).wait_send()
+            give_scale(t).wait_send()
 
     for t in range(1, shards):
         for i in range(2):
@@ -367,11 +399,11 @@
     dma = pltpu.SemaphoreType.DMA
     anywhere = pl.BlockSpec(memory_space=pl.ANY)
     scalars = pl.BlockSpec(memory_space=pltpu.SMEM)
-    return pl.pallas_call(
+    moved, scales = pl.pallas_call(
         functools.partial(kernel, reps, shards, chunks),
-        out_shape=jax.ShapeDtypeStruct((rows_dev, cols), BF16),
+        out_shape=(pltpu.VMEM((rows_dev, cols), BF16), pltpu.VMEM((8, cols), F32)),
         in_specs=[scalars, scalars, anywhere, anywhere],
-        out_specs=anywhere,
+        out_specs=(pl.BlockSpec(memory_space=pltpu.VMEM), pl.BlockSpec(memory_space=pltpu.VMEM)),
         scratch_shapes=[
             pltpu.VMEM((rows_dev, all_cols), BF16),
             pltpu.VMEM((chunks, hops, step, cols), BF16),
@@ -386,13 +418,16 @@
             pltpu.VMEM((shards, rows_dev, width), BF16),
             pltpu.VMEM((2, blocks, rows_dev, width), BF16),
             pltpu.VMEM((2, shards, rows_dev, width), BF16),
-            dma((4,)),
+            pltpu.VMEM((8, width), F32),
+            dma((5,)),
             dma((chunks, hops)),
             dma((chunks, hops)),
             dma((chunks, hops)),
             dma((chunks, hops)),
             dma((chunks, blocks)),
             dma((chunks, shards)),
+            dma((shards,)),
+            dma((blocks,)),
             dma((shards,)),
             dma((blocks,)),
             dma((2, shards)),
@@ -404,6 +439,7 @@
             collective_id=0, has_side_effects=True, vmem_limit_bytes=60 * 1024 * 1024
         ),
     )(owner_plan, refresh, grad_parts[0], roots[0, 0])
+    return (moved.astype(F32) * scales[:1]).astype(BF16)
 
 
 def solution(mesh):

time: 38 us -> 37.7 us (level)
  local copies, waits for them, and re-layouts: 1.67 us -> 0.01 us
  other arithmetic: 0 us -> 0.75 us
  Pallas kernels: 36.2 us -> 36.8 us
    unnamed x1 -> x0, local copies, waits for them, and re-layouts: 1.67 us -> none
    convert_element_type x0 -> x1, other arithmetic: none -> 0.75 us  [local(): return (moved.astype(F32) * scales[:1]).astype(BF16)]
    pallas_call x1, Pallas kernels: 36.2 us -> 36.8 us  [local(): pl.pallas_call(functools.partial(kernel, reps, shards, chunks), out_shape...]
where the time goes in v5:
time: 37.7 us; the launch traced here: 37.6 us
  Pallas kernels  36.8 us (98%)
  other arithmetic  0.75 us (2%)
    pallas_call x1, Pallas kernels, local(): pl.pallas_call(functools.partial(kernel, reps, shards, chunks), out_shape...  36.8 us

profile of v5, /device:TPU:0, one launch (start us, length us, event | category | flops | bytes accessed | tf_op | source)
XLA Modules:
  0.0 37.6 jit_solution(13998616658941095829)
XLA Ops:
  0.0 36.8 %shard_map.46 = (bf16[64,2048]{1,0:T(8,128)(2,1)S(1)}, f32[8,2048]{1,0:T(8,128)S(1)}) custom-call(s32[1,4]{1,0:T(1,128)} %owner.1, s32[1,2]{1,0:T(1,128)} %refresh.1, bf16[64,8192]{1,0:T(8,128)(2,1)} %bitcast.3, bf16[2,512,512]{2,1,0:T(8,128)(2,1)} %bitcast.4), custom_call_target="tpu_custom_call" | custom-call | tf_op jit(solution)/shard_map/pallas_call | solution.py:402
  36.8 0.8 %multiply_convert_fusion = bf16[64,2048]{1,0:T(8,128)(2,1)} fusion(bf16[64,2048]{1,0:T(8,128)(2,1)S(1)} %get-tuple-element.7, f32[2048]{0:T(1024)S(1)} %bitcast.5), kind=kLoop, calls=%fused_computation | loop fusion | flops 393216 | bytes 532480 | tf_op jit(solution)/shard_map/convert_element_type | solution.py:442
  (1 shorter events, 0.0 us)
